TPU v7x, 512 devices: a whole 4x8x8 slice. The times are simulated.
512 devices in a mesh: gx: 64 (over y, x, z_hi), ba: 8 (over z_lo, core).
Axes of the slice: x: 4, y: 8, z: 8 (z_hi: 2, z_lo: 4; z = z_hi * 4 + z_lo), core: 2. Of those that a mesh axis runs over, the one named last changes fastest.
Arguments:
- density: float32 [64, 128, 64, 128], P('ba', 'gx'), may hold values from 0.2 to 2
- diffusivity: float32 [64], P('ba'), may hold values from 0.03 to 0.16
- positions: int32 [512], replicated, may hold values from 0 to 1048575
- spectrum: float32 [512, 64], P(None, 'ba'), may hold values from 0.3 to 3
- cell_class: int32 [128, 64, 128], P('gx', 'ba'), may hold values from 0 to 63, as said below
- operators: bfloat16 [64, 64, 64], replicated, as said below
Outputs:
- updated: float32 [64, 128, 64, 128], P(None, 'gx', 'ba')
Inputs may be any that keep to these rules, and one draw needn't show every extreme that they name: `cell_class`: among the cells of one device (x planes of one index of gx, y rows of one index of ba) no class appears more than 64 times, and on every device some class appears exactly 64 times. `operators`: each matrix has positive diagonal entries and full rank.
All inputs are finite; a program needn't handle non-finite values.
Results may differ from a plain program's by a relative error of at most 0.003.
Values may be sent and summed in bfloat16 or wider, within the bound.
A program may use at most 64 MiB of HBM per device.

v0:
```python
import math

import jax
import jax.numpy as jnp
from jax import lax
from jax.sharding import PartitionSpec as P


def extended(cells, sides, width):
    for axis, dim in sides:
        count = lax.axis_size(axis)
        head = lax.slice_in_dim(cells, 0, width, axis=dim)
        tail = lax.slice_in_dim(cells, cells.shape[dim] - width, cells.shape[dim], axis=dim)
        cells = jnp.concatenate(
            [
                lax.ppermute(tail, axis, [(i, (i + 1) % count) for i in range(count)]),
                cells,
                lax.ppermute(head, axis, [((i + 1) % count, i) for i in range(count)]),
            ],
            axis=dim,
        )
    return cells


def laplace_inner(padded):
    centre = padded[:, 1:-1]
    result = padded[:, 2:] + padded[:, :-2] - 6.0 * centre
    result = result + jnp.roll(centre, 1, 2) + jnp.roll(centre, -1, 2)
    return result + jnp.roll(centre, 1, 3) + jnp.roll(centre, -1, 3)


def source_planes(positions, spectrum, first_plane, plane_count, width_x, grid_y, grid_z):
    plane_size = grid_y * grid_z
    plane_of = positions // plane_size
    remainder = positions - plane_of * plane_size
    offset = jnp.mod(plane_of - first_plane, width_x)
    location = jnp.where(
        offset < plane_count, offset * plane_size + remainder, plane_count * plane_size
    )
    flat_source = jnp.zeros((spectrum.shape[1], plane_count * plane_size), jnp.float32)
    flat_source = flat_source.at[:, location].add(spectrum.T, mode="drop")
    return flat_source.reshape(spectrum.shape[1], plane_count, grid_y, grid_z)


def body(density, diffusivity, positions, spectrum, cell_class, operators):
    planes_dev = density.shape[1]
    grid_y = density.shape[2]
    grid_z = density.shape[3]
    width_x = planes_dev * lax.axis_size("gx")
    first_plane = lax.axis_index("gx") * planes_dev
    diffusion = diffusivity[:, None, None, None]
    wide_source = source_planes(
        positions, spectrum, first_plane - 1, planes_dev + 2, width_x, grid_y, grid_z
    )
    padded = extended(density, (("gx", 1),), 2)
    middle = padded[:, 1:-1] + diffusion * laplace_inner(padded) + wide_source
    current = middle[:, 1:-1] + diffusion * laplace_inner(middle) + wide_source[:, 1:-1]
    rounded = current.astype(jnp.bfloat16)
    cell_field = lax.all_to_all(rounded, "ba", split_axis=2, concat_axis=0, tiled=True)
    bins_all = cell_field.shape[0]
    flat_cells = cell_field.reshape(bins_all, -1)
    classes = cell_class.reshape(-1)
    cell_total = classes.shape[0]
    class_count = operators.shape[0]
    class_range = jnp.arange(class_count, dtype=jnp.int32)
    block_size = math.gcd(cell_total, 512)
    block_count = cell_total // block_size
    weights_flat = jnp.transpose(operators, (1, 0, 2)).reshape(bins_all, class_count * bins_all)
    blocks = jnp.transpose(flat_cells.reshape(bins_all, block_count, block_size), (1, 0, 2))
    label_blocks = classes.reshape(block_count, block_size)

    def one_block(block_pair):
        values, labels = block_pair
        onehot = (labels[None, :] == class_range[:, None]).astype(jnp.bfloat16)
        spread = (onehot[:, None, :] * values[None, :, :]).reshape(
            class_count * bins_all, block_size
        )
        return jnp.dot(weights_flat, spread, preferred_element_type=jnp.float32)

    mapped = lax.map(one_block, (blocks, label_blocks))
    output = jnp.transpose(mapped, (1, 0, 2)).reshape(bins_all, cell_total)
    return output.reshape(cell_field.shape)


def solution(mesh):
    in_specs = (P("ba", "gx", None, None), P("ba"), P(), P(None, "ba"), P("gx", "ba", None), P())
    out_specs = P(None, "gx", "ba", None)
    return jax.shard_map(body, mesh=mesh, in_specs=in_specs, out_specs=out_specs, check_vma=False)
```

profile of v0, /device:TPU:6, one launch (start us, length us, event | category | flops | bytes accessed | tf_op | source)
XLA Modules:
  0.0 86.1 jit_solution(7964898329634870951)
XLA Ops:
  0.0 10.9 %collective-permute-start = (f32[8,2,64,128]{3,2,1,0:T(8,128)}, f32[8,2,64,128]{3,2,1,0:T(8,128)S(1)}, u32[]{:S(2)}, u32[]{:S(2)}) collective-permute-start(f32[8,2,64,128]{3,2,1,0:T(8,128)} %param.8), channel_id=1, source_target_pairs={{0,8},{8,16},{16,24},{24,32},{32,40},{40,48},{48,56},{56,64},{64,7... | collective-permute-start | bytes 1572872 | tf_op jit(solution)/shard_map/ppermute | solution.py:16
  10.9 2.2 %collective-permute-start.1 = (f32[8,2,64,128]{3,2,1,0:T(8,128)}, f32[8,2,64,128]{3,2,1,0:T(8,128)S(1)}, u32[]{:S(2)}, u32[]{:S(2)}) collective-permute-start(f32[8,2,64,128]{3,2,1,0:T(8,128)} %param.8), channel_id=1, source_target_pairs={{8,0},{16,8},{24,16},{32,24},{40,32},{48,40},{56,48},{64,56},{72,6... | collective-permute-start | bytes 1572872 | tf_op jit(solution)/shard_map/ppermute | solution.py:18
  13.1 0.8 copy.31
  14.0 0.7 compare_select_fusion
  14.7 9.0 %scatter_custom_fusion = f32[8,32768]{0,1:T(8,128)} fusion(s32[512]{0:T(512)S(1)} %compare_select_fusion, f32[512,8]{1,0:T(8,128)S(1)} %copy.31, f32[]{:T(128)} %constant.52.clone.1), kind=kCustom, calls=%fused_computation.9 | custom fusion | flops 4096 | bytes 1048580 | tf_op jit(solution)/shard_map/scatter-add | solution.py:41
  23.7 9.9 %copy.32 = f32[8,4,64,128]{3,2,1,0:T(8,128)S(1)} copy(f32[8,4,64,128]{0,3,2,1:T(8,128)} %bitcast.35) | data formatting | bytes 2097152 | tf_op jit(solution)/shard_map/reshape | solution.py:42
  33.7 23.6 %collective-permute-done.1 = f32[8,2,64,128]{3,2,1,0:T(8,128)S(1)} collective-permute-done((f32[8,2,64,128]{3,2,1,0:T(8,128)}, f32[8,2,64,128]{3,2,1,0:T(8,128)S(1)}, u32[]{:S(2)}, u32[]{:S(2)}) %collective-permute-start.1) | collective-permute-done | bytes 524320 | tf_op jit(solution)/shard_map/ppermute | solution.py:18
  57.6 0.4 fusion.25
  58.0 0.4 fusion.26
  58.7 1.2 %fusion.13 = f32[8,4,64,128]{3,2,1,0:T(8,128)S(1)} fusion(f32[8,4,64,128]{3,2,1,0:T(8,128)S(1)} %copy.32, f32[8,2,64,128]{3,2,1,0:T(8,128)S(1)} %collective-permute-done.1, f32[8,2,64,128]{3,2,1,0:T(8,128)S(1)} %copy-done, f32[8,2,64,128]{3,2,1,0:T(8,128)S(1)} %collective-permute-done, f32[8,4,63,128]{3,2,1,0:T(8,128)S(1)} %get-tuple-element.80, ...), kind=kLoop, calls=%fused_computation.19 | loop fusion | flops 4194304 | bytes 8912928 | tf_op jit(solution)/shard_map/add | solution.py:56
  60.4 0.6 fusion.14
  61.0 0.9 %copy.34 = bf16[8,2,64,128]{3,0,1,2:T(8,128)(2,1)} copy(bf16[8,2,64,128]{3,2,1,0:T(8,128)(2,1)S(1)} %fusion.14) | data formatting | bytes 524288 | tf_op jit(solution)/shard_map/convert_element_type | solution.py:58
  61.8 8.2 %all-to-all-start = ((bf16[8,2,64,128]{3,0,1,2:T(8,128)(2,1)}), bf16[8,2,64,128]{3,0,1,2:T(8,128)(2,1)S(1)}, u32[]{:S(2)}, u32[]{:S(2)}) async-start(bf16[8,2,64,128]{3,0,1,2:T(8,128)(2,1)} %copy.34), calls=%async_computation | async-start | bytes 524288 | tf_op jit(solution)/shard_map/all_to_all | solution.py:59
  70.0 0.7 copy.36
  70.7 0.8 reshape.38
  71.5 8.2 %all-to-all-done = bf16[8,2,64,128]{3,0,1,2:T(8,128)(2,1)S(1)} async-done(((bf16[8,2,64,128]{3,0,1,2:T(8,128)(2,1)}), bf16[8,2,64,128]{3,0,1,2:T(8,128)(2,1)S(1)}, u32[]{:S(2)}, u32[]{:S(2)}) %all-to-all-start) | async-done | bytes 262176 | tf_op jit(solution)/shard_map/all_to_all | solution.py:59
  80.0 4.8 %while.11 = (s32[]{:T(128)}, f32[4,64,512]{2,1,0:T(8,128)S(1)}, s32[4,512]{1,0:T(4,128)S(1)}, bf16[4,64,512]{2,1,0:T(8,128)(2,1)S(1)}, bf16[64,4096]{1,0:T(8,128)(2,1)S(1)}, /*index=5*/s32[]{:T(128)}) while((s32[]{:T(128)}, f32[4,64,512]{2,1,0:T(8,128)S(1)}, s32[4,512]{1,0:T(4,128)S(1)}, bf16[4,64,512]{2,1,0:T(8,128)(2,1)S(1)}, ...), condition=%wide.region_2.3_spmd.clone, body=%wide.region_1.2_spmd.clone.sunk | while | flops 270598144 | bytes 9377881 | solution.py:80
  80.0 0.3 broadcast_multiply_fusion.2
  80.3 0.8 fusion.42
  81.5 0.8 fusion.42
  82.7 0.8 fusion.42
  83.9 0.8 fusion.42
  84.8 0.3 copy.38
  85.1 1.0 %reshape_reshape.11 = f32[64,2,8,128]{3,2,1,0:T(8,128)} reshape(f32[64,4,512]{2,1,0:T(4,128)S(1)} %copy.38) | data formatting | bytes 1048576 | tf_op jit(solution)/shard_map/reshape;reshape | solution.py:82
  (38 shorter events, 2.4 us)
Async XLA Ops:
  0.0 33.6 %collective-permute-start = (f32[8,2,64,128]{3,2,1,0:T(8,128)}, f32[8,2,64,128]{3,2,1,0:T(8,128)S(1)}, u32[]{:S(2)}, u32[]{:S(2)}) collective-permute-start(f32[8,2,64,128]{3,2,1,0:T(8,128)} %param.8), channel_id=1, source_target_pairs={{0,8},{8,16},{16,24},{24,32},{32,40},{40,48},{48,56},{56,64},{64,7... | collective-permute-start | bytes 1572872 | tf_op jit(solution)/shard_map/ppermute | solution.py:16
  10.9 46.4 %collective-permute-start.1 = (f32[8,2,64,128]{3,2,1,0:T(8,128)}, f32[8,2,64,128]{3,2,1,0:T(8,128)S(1)}, u32[]{:S(2)}, u32[]{:S(2)}) collective-permute-start(f32[8,2,64,128]{3,2,1,0:T(8,128)} %param.8), channel_id=1, source_target_pairs={{8,0},{16,8},{24,16},{32,24},{40,32},{48,40},{56,48},{64,56},{72,6... | collective-permute-start | bytes 1572872 | tf_op jit(solution)/shard_map/ppermute | solution.py:18
  23.7 9.9 %copy-start = (f32[8,2,64,128]{3,2,1,0:T(8,128)S(1)}, f32[8,2,64,128]{3,2,1,0:T(8,128)}, u32[]{:S(2)}) copy-start(f32[8,2,64,128]{3,2,1,0:T(8,128)} %param.8) | copy-start | bytes 1572868
  58.0 0.7 copy-start.3
  60.4 9.6 %copy-start.2 = (s32[2,8,128]{2,1,0:T(8,128)S(1)}, s32[2,8,128]{2,1,0:T(8,128)}, u32[]{:S(2)}) copy-start(s32[2,8,128]{2,1,0:T(8,128)} %param.12) | copy-start | bytes 24580
  60.9 9.1 %copy-start.1 = (bf16[64,64,64]{2,1,0:T(8,128)(2,1)S(1)}, bf16[64,64,64]{2,1,0:T(8,128)(2,1)}, u32[]{:S(2)}) copy-start(bf16[64,64,64]{2,1,0:T(8,128)(2,1)} %param.13) | copy-start | bytes 1572868
  61.8 17.9 %all-to-all-start = ((bf16[8,2,64,128]{3,0,1,2:T(8,128)(2,1)}), bf16[8,2,64,128]{3,0,1,2:T(8,128)(2,1)S(1)}, u32[]{:S(2)}, u32[]{:S(2)}) async-start(bf16[8,2,64,128]{3,0,1,2:T(8,128)(2,1)} %copy.34), calls=%async_computation | async-start | bytes 524288 | tf_op jit(solution)/shard_map/all_to_all | solution.py:59
where the time goes:
time: 86.5 us; the launch traced here: 86.1 us
  waiting for transfers between devices  31.8 us (37%)
  starting transfers between devices  21.2 us (25%)
  local copies, waits for them, and re-layouts  16.6 us (19%)
  other arithmetic  12.6 us (15%)
  matrix products  3.33 us (4%)
    ppermute x1, waiting for transfers between devices, extended(): lax.ppermute(head, axis, [((i + 1) % count, i) for i in range(count)])  23.6 us
    ppermute x1, starting transfers between devices, extended(): lax.ppermute(tail, axis, [(i, (i + 1) % count) for i in range(count)])  10.9 us
    reshape x1, local copies, waits for them, and re-layouts, source_planes(): return flat_source.reshape(spectrum.shape[1], plane_count, grid_y, grid_z)  9.86 us
    scatter-add x1, other arithmetic, source_planes(): flat_source = flat_source.at[:, location].add(spectrum.T, mode='drop')  9.02 us
    all_to_all x1, waiting for transfers between devices, body(): lax.all_to_all(rounded, 'ba', split_axis=2, concat_axis=0, tiled=True)  8.21 us
    all_to_all x1, starting transfers between devices, body(): lax.all_to_all(rounded, 'ba', split_axis=2, concat_axis=0, tiled=True)  8.15 us
    dot_general x4, matrix products, one_block(): return jnp.dot(weights_flat, spread, preferred_element_type=jnp.float32)  3.33 us
    ppermute x1, starting transfers between devices, extended(): lax.ppermute(head, axis, [((i + 1) % count, i) for i in range(count)])  2.19 us
  transfers between devices with their start and end apart: 3, of which 2 were waited for; matrix products, arithmetic and copies ran while one was open for 26% of the time, Pallas kernels for 0%

commit v1 on v0

v1 whole, which is shorter than its diff:
```python
import functools

import jax
import jax.numpy as jnp
from jax import lax
from jax.experimental import pallas as pl
from jax.experimental.pallas import tpu as pltpu
from jax.sharding import PartitionSpec as P

MESH = pl.DeviceIdType.MESH

LOW = 0.1
STEPS = 32767.0
BIAS = 32768


def encode(rho):
    return ((rho - LOW) * STEPS + 0.5).astype(jnp.int32) - BIAS


def decode(code):
    return code.astype(jnp.int32).astype(jnp.float32) * (1.0 / STEPS) + (LOW + BIAS / STEPS)


def yz_sum(field):
    return (
        pltpu.roll(field, 1, 0)
        + pltpu.roll(field, field.shape[0] - 1, 0)
        + pltpu.roll(field, 1, 1)
        + pltpu.roll(field, field.shape[1] - 1, 1)
    )


def kernel(
    gx_count,
    ba_count,
    diff_ref,
    density_ref,
    pos_ref,
    spec_ref,
    class_ref,
    oper_ref,
    out_ref,
    dens,
    stage,
    held,
    halo,
    parm_out,
    parm,
    source,
    rounded,
    gathered,
    wide,
    opers,
    weights,
    load_sem,
    swap_send,
    swap_recv,
    parm_send,
    parm_recv,
    halo_send,
    halo_recv,
    spread_send,
    spread_recv,
):
    bins_dev, planes, rows_y, grid_z = density_ref.shape
    half = bins_dev // 2
    ring = 2 * ba_count
    rows_dev = rows_y // ba_count
    bins_all = gathered.shape[0]
    remnants = pos_ref.shape[1]
    part = remnants // 2
    gx = lax.axis_index("gx")
    ba = lax.axis_index("ba")
    side = lax.rem(gx, 2)
    column = gx - side
    me = side * ba_count + ba
    meet = lax.rem(ba + ba_count // 2, ba_count)
    right = lax.rem(gx + 2, gx_count)
    left = lax.rem(gx + gx_count - 2, gx_count)

    load_density = [
        pltpu.make_async_copy(
            density_ref.at[pl.ds(h * half, half)], dens.at[pl.ds(h * half, half)], load_sem.at[h]
        )
        for h in range(2)
    ]
    for copy in load_density:
        copy.start()
    load_opers = pltpu.make_async_copy(oper_ref, opers, load_sem.at[2])
    load_opers.start()

    barrier = pltpu.get_barrier_semaphore()
    for offset in range(1, ring):
        peer = lax.rem(me + offset, ring)
        pl.semaphore_signal(
            barrier,
            inc=1,
            device_id=(column + peer // ba_count, lax.rem(peer, ba_count)),
            device_id_type=MESH,
        )
    for other in (left, right):
        pl.semaphore_signal(barrier, inc=1, device_id=(other, ba), device_id_type=MESH)

    bin_row = lax.broadcasted_iota(jnp.int32, (half, grid_z), 0)
    for h in range(2):
        parm_out[h, :, 0:part] = spec_ref[
            h * half : (h + 1) * half, pl.ds(pl.multiple_of(side * part, part), part)
        ]
        value = jnp.zeros((half, grid_z), jnp.float32)
        for b in range(half):
            value = jnp.where(bin_row == b, diff_ref[h * half + b], value)
        parm_out[h, :, part:] = value
    for h in range(2):
        load_density[h].wait()
        for b in range(half):
            stage[h, b] = encode(dens[h * half + b]).astype(jnp.int16)

    pl.semaphore_wait(barrier, ring + 1)

    swaps = []
    parms = []
    for h in range(2):
        target = (column + h, meet)
        parms.append(
            pltpu.make_async_remote_copy(
                src_ref=parm_out.at[h],
                dst_ref=parm.at[side],
                send_sem=parm_send.at[h],
                recv_sem=parm_recv.at[side],
                device_id=target,
                device_id_type=MESH,
            )
        )
        parms[h].start()
    for b in range(half):
        for h in range(2):
            swaps.append(
                pltpu.make_async_remote_copy(
                    src_ref=stage.at[h, b],
                    dst_ref=held.at[side, b],
                    send_sem=swap_send.at[h, b],
                    recv_sem=swap_recv.at[side, b],
                    device_id=(column + h, meet),
                    device_id_type=MESH,
                )
            )
            swaps[-1].start()

    load_opers.wait()
    groups = weights.shape[0] // bins_all
    per_group = weights.shape[1] // bins_all

    def arrange(a, carry):
        weights[pl.ds(pl.multiple_of(a * bins_all, bins_all), bins_all), :] = jnp.concatenate(
            [opers[a * per_group + j] for j in range(per_group)], axis=1
        )
        return carry

    lax.fori_loop(0, groups, arrange, 0)

    def wait_parm(s):
        pltpu.make_async_copy(parm.at[s], parm.at[s], parm_recv.at[s]).wait()

    wait_parm(0)
    wait_parm(1)
    planes_col = 2 * planes
    planes_src = planes_col + 2
    pos = pos_ref[...]
    pos_x = pos // (rows_y * grid_z)
    pos_y = lax.rem(pos // grid_z, rows_y)
    pos_z = lax.rem(pos, grid_z)
    width = gx_count * planes
    pos_x = lax.rem(pos_x + (width + 1) - column * planes, width)
    pos_row = pos_x * rows_y + pos_y
    is_row = lax.broadcasted_iota(jnp.int32, (planes_src * rows_y, remnants), 0) == pos_row
    is_z = lax.broadcasted_iota(jnp.int32, (grid_z, remnants), 0) == pos_z
    is_z = jnp.where(is_z, 1.0, 0.0).astype(jnp.bfloat16)
    for b in range(half):
        spec = jnp.concatenate([parm[0, b : b + 1, 0:part], parm[1, b : b + 1, 0:part]], axis=1)
        high = spec.astype(jnp.bfloat16).astype(jnp.float32)
        low = spec - high
        total = jnp.zeros((planes_src * rows_y, grid_z), jnp.float32)
        for piece in (high, low):
            total += lax.dot_general(
                jnp.where(is_row, piece, 0.0).astype(jnp.bfloat16),
                is_z,
                (((1,), (1,)), ((), ())),
                preferred_element_type=jnp.float32,
            )
        source[b] = total.reshape(planes_src, rows_y, grid_z)

    halos = [[None, None] for _ in range(half)]

    def forward(b):
        for s in range(2):
            pltpu.make_async_copy(held.at[s, b], held.at[s, b], swap_recv.at[s, b]).wait()
            halos[b][s] = pltpu.make_async_remote_copy(
                src_ref=held.at[s, b],
                dst_ref=halo.at[s, b],
                send_sem=halo_send.at[s, b],
                recv_sem=halo_recv.at[s, b],
                device_id=(left if s == 0 else right, ba),
                device_id_type=MESH,
            )
            halos[b][s].start()

    def diffuse(b):
        for s in range(2):
            halos[b][s].wait_recv()
        rate = parm[0, b : b + 1, part:]
        centre = 1.0 - 6.0 * rate
        fields = [decode(halo[1, b, p]) for p in range(planes)]
        fields += [decode(held[s, b, p]) for s in range(2) for p in range(planes)]
        fields += [decode(halo[0, b, p]) for p in range(planes)]
        sources = [source[b, p] for p in range(planes_src)]
        first = [
            centre * fields[p + 1] + rate * (fields[p] + fields[p + 2] + yz_sum(fields[p + 1])) + sources[p]
            for p in range(planes_src)
        ]
        second = [
            centre * first[p + 1]
            + rate * (first[p] + first[p + 2] + yz_sum(first[p + 1]))
            + sources[p + 1]
            for p in range(planes_col)
        ]
        for s in range(2):
            block = jnp.concatenate(
                [second[s * planes + p].reshape(ba_count, rows_dev, grid_z) for p in range(planes)],
                axis=1,
            )
            rounded[b, pl.ds(s * ba_count, ba_count)] = block.astype(jnp.bfloat16)

    group = 2 * meet + side

    def spread(b):
        slot = gathered.at[group * half + b]
        for offset in list(range(ring // 2, ring)) + list(range(1, ring // 2)):
            peer = lax.rem(me + offset, ring)
            pltpu.make_async_remote_copy(
                src_ref=rounded.at[b, peer],
                dst_ref=slot,
                send_sem=spread_send,
                recv_sem=spread_recv,
                device_id=(column + peer // ba_count, lax.rem(peer, ba_count)),
                device_id_type=MESH,
            ).start()
        pltpu.make_async_copy(rounded.at[b, me], slot, spread_recv).start()

    forward(0)
    for b in range(half):
        if b + 1 < half:
            forward(b + 1)
        diffuse(b)
        spread(b)

    pltpu.make_async_copy(gathered, gathered, spread_recv).wait()

    wide[...] = gathered[...].astype(jnp.float32).reshape(wide.shape)
    cells = planes * rows_dev

    def update(step, carry):
        first_row = 2 * step
        values = jnp.concatenate(
            [wide[pl.ds(first_row + j, bins_all, stride=cells), :] for j in range(2)], axis=1
        )
        classes = jnp.concatenate([class_ref[pl.ds(first_row + j, 1), :] for j in range(2)], axis=1)
        within = lax.rem(classes, per_group)
        outer = classes // per_group
        stacked = jnp.concatenate(
            [jnp.where(within == j, values, 0.0) for j in range(per_group)], axis=0
        ).astype(jnp.bfloat16)
        products = jnp.dot(weights[...], stacked, preferred_element_type=jnp.float32)
        result = products[0:bins_all]
        for a in range(1, groups):
            result = jnp.where(outer == a, products[a * bins_all : (a + 1) * bins_all], result)
        for j in range(2):
            out_ref[pl.ds(first_row + j, bins_all, stride=cells), :] = result[
                :, j * grid_z : (j + 1) * grid_z
            ]
        return carry

    lax.fori_loop(0, cells // 2, update, 0)

    for copy in parms + swaps:
        copy.wait_send()
    for b in range(half):
        for s in range(2):
            halos[b][s].wait_send()
    sent = rounded.at[:, pl.ds(0, ring - 1)]
    pltpu.make_async_copy(sent, sent, spread_send).wait()


def solution(mesh):
    gx_count, ba_count = mesh.shape["gx"], mesh.shape["ba"]

    def step(density, diffusivity, positions, spectrum, cell_class, operators):
        bins_dev, planes, rows_y, grid_z = density.shape
        classes, bins_all, _ = operators.shape
        remnants = positions.shape[0]
        half = bins_dev // 2
        cells = planes * (rows_y // ba_count)
        per_group = 4
        vmem = pl.BlockSpec(memory_space=pltpu.VMEM)
        anywhere = pl.BlockSpec(memory_space=pl.ANY)
        out = pl.pallas_call(
            functools.partial(kernel, gx_count, ba_count),
            out_shape=jax.ShapeDtypeStruct((bins_all * cells, grid_z), jnp.float32),
            in_specs=[
                pl.BlockSpec(memory_space=pltpu.SMEM),
                anywhere,
                vmem,
                vmem,
                vmem,
                anywhere,
            ],
            out_specs=vmem,
            scratch_shapes=[
                pltpu.VMEM(density.shape, jnp.float32),
                pltpu.VMEM((2, half, planes, rows_y, grid_z), jnp.int16),
                pltpu.VMEM((2, half, planes, rows_y, grid_z), jnp.int16),
                pltpu.VMEM((2, half, planes, rows_y, grid_z), jnp.int16),
                pltpu.VMEM((2, half, remnants // 2 + grid_z), jnp.float32),
                pltpu.VMEM((2, half, remnants // 2 + grid_z), jnp.float32),
                pltpu.VMEM((half, 2 * planes + 2, rows_y, grid_z), jnp.float32),
                pltpu.VMEM((half, 2 * ba_count, cells, grid_z), jnp.bfloat16),
                pltpu.VMEM((bins_all, cells, grid_z), jnp.bfloat16),
                pltpu.VMEM((bins_all * cells, grid_z), jnp.float32),
                pltpu.VMEM(operators.shape, jnp.bfloat16),
                pltpu.VMEM((classes // per_group * bins_all, per_group * bins_all), jnp.bfloat16),
                pltpu.SemaphoreType.DMA((3,)),
                pltpu.SemaphoreType.DMA((2, half)),
                pltpu.SemaphoreType.DMA((2, half)),
                pltpu.SemaphoreType.DMA((2,)),
                pltpu.SemaphoreType.DMA((2,)),
                pltpu.SemaphoreType.DMA((2, half)),
                pltpu.SemaphoreType.DMA((2, half)),
                pltpu.SemaphoreType.DMA,
                pltpu.SemaphoreType.DMA,
            ],
            compiler_params=pltpu.CompilerParams(collective_id=0, has_side_effects=True),
        )(
            diffusivity,
            density,
            positions.reshape(1, remnants),
            spectrum.T,
            cell_class.reshape(cells, grid_z),
            operators,
        )
        return out.reshape(bins_all, planes, rows_y // ba_count, grid_z)

    in_specs = (P("ba", "gx", None, None), P("ba"), P(), P(None, "ba"), P("gx", "ba", None), P())
    return jax.shard_map(
        step, mesh=mesh, in_specs=in_specs, out_specs=P(None, "gx", "ba", None), check_vma=False
    )
```

time: 86.5 us -> 41.8 us (0.48)
  the two profiles are of different devices: /device:TPU:6 before, /device:TPU:1 now
where the time goes in v1:
time: 41.8 us; the launch traced here: 41.5 us
  Pallas kernels  39.7 us (95%)
  local copies, waits for them, and re-layouts  1.87 us (4%)
    pallas_call x1, Pallas kernels, step(): pl.pallas_call(functools.partial(kernel, gx_count, ba_count), out_shape=j...  39.7 us
    unnamed x1, local copies, waits for them, and re-layouts  1.87 us

profile of v1, /device:TPU:1, one launch (start us, length us, event | category | flops | bytes accessed | tf_op | source)
XLA Modules:
  0.0 41.5 jit_solution(15347119474486950019)
XLA Ops:
  0.0 39.7 %shard_map.64 = f32[1024,128]{1,0:T(8,128)} custom-call(f32[8]{0:T(128)} %diff_ref.1, f32[8,2,64,128]{3,2,1,0:T(8,128)} %density_ref.1, s32[1,512]{1,0:T(1,128)} %bitcast.7, f32[8,512]{1,0:T(8,128)} %bitcast.5, s32[16,128]{1,0:T(8,128)} %bitcast.6, bf16[64,64,64]{2,1,0:T(8,128)(2,1)} %oper_ref.1), custom_call_target="tpu_custom_call" | custom-call | tf_op jit(solution)/shard_map/pallas_call | solution.py:306
  39.7 1.9 %copy.8 = f32[64,2,8,128]{3,2,1,0:T(8,128)} copy(f32[64,2,8,128]{3,2,1,0:T(8,128)} %bitcast.4) | data formatting | bytes 1048576

commit v2 on v1

--- a/solution.py
+++ b/solution.py
@@ -12,6 +12,8 @@
 LOW = 0.1
 STEPS = 32767.0
 BIAS = 32768
+
+DEPTH = 2
 
 
 def encode(rho):
@@ -34,13 +36,17 @@
 def kernel(
     gx_count,
     ba_count,
+    diff_hbm,
+    density_ref,
+    pos_hbm,
+    spec_hbm,
+    class_hbm,
+    oper_ref,
+    out_ref,
     diff_ref,
-    density_ref,
     pos_ref,
     spec_ref,
     class_ref,
-    oper_ref,
-    out_ref,
     dens,
     stage,
     held,
@@ -79,29 +85,41 @@
     right = lax.rem(gx + 2, gx_count)
     left = lax.rem(gx + gx_count - 2, gx_count)
 
-    load_density = [
-        pltpu.make_async_copy(
-            density_ref.at[pl.ds(h * half, half)], dens.at[pl.ds(h * half, half)], load_sem.at[h]
-        )
-        for h in range(2)
-    ]
-    for copy in load_density:
-        copy.start()
-    load_opers = pltpu.make_async_copy(oper_ref, opers, load_sem.at[2])
-    load_opers.start()
-
     barrier = pltpu.get_barrier_semaphore()
-    for offset in range(1, ring):
-        peer = lax.rem(me + offset, ring)
-        pl.semaphore_signal(
-            barrier,
-            inc=1,
-            device_id=(column + peer // ba_count, lax.rem(peer, ba_count)),
-            device_id_type=MESH,
-        )
+    greetings = 0
+    for chips in (0, 1, 2, ring // 2 - 2, ring // 2 - 1):
+        for core in range(2):
+            if chips or core:
+                peer = 2 * lax.rem(me // 2 + chips, ring // 2) + lax.rem(me + core, 2)
+                pl.semaphore_signal(
+                    barrier,
+                    inc=1,
+                    device_id=(column + peer // ba_count, lax.rem(peer, ba_count)),
+                    device_id_type=MESH,
+                )
+                greetings += 1
     for other in (left, right):
         pl.semaphore_signal(barrier, inc=1, device_id=(other, ba), device_id_type=MESH)
-
+        greetings += 1
+
+    loads = [
+        pltpu.make_async_copy(diff_hbm, diff_ref, load_sem.at[0]),
+        pltpu.make_async_copy(spec_hbm, spec_ref, load_sem.at[1]),
+        pltpu.make_async_copy(
+            density_ref.at[pl.ds(0, half)], dens.at[pl.ds(0, half)], load_sem.at[2]
+        ),
+        pltpu.make_async_copy(
+            density_ref.at[pl.ds(half, half)], dens.at[pl.ds(half, half)], load_sem.at[3]
+        ),
+        pltpu.make_async_copy(pos_hbm, pos_ref, load_sem.at[4]),
+        pltpu.make_async_copy(oper_ref, opers, load_sem.at[5]),
+        pltpu.make_async_copy(class_hbm, class_ref, load_sem.at[6]),
+    ]
+    for copy in loads:
+        copy.start()
+
+    loads[0].wait()
+    loads[1].wait()
     bin_row = lax.broadcasted_iota(jnp.int32, (half, grid_z), 0)
     for h in range(2):
         parm_out[h, :, 0:part] = spec_ref[
@@ -112,11 +130,11 @@
             value = jnp.where(bin_row == b, diff_ref[h * half + b], value)
         parm_out[h, :, part:] = value
     for h in range(2):
-        load_density[h].wait()
+        loads[2 + h].wait()
         for b in range(half):
             stage[h, b] = encode(dens[h * half + b]).astype(jnp.int16)
 
-    pl.semaphore_wait(barrier, ring + 1)
+    pl.semaphore_wait(barrier, greetings)
 
     swaps = []
     parms = []
@@ -133,7 +151,7 @@
             )
         )
         parms[h].start()
-    for b in range(half):
+    def swap(b):
         for h in range(2):
             swaps.append(
                 pltpu.make_async_remote_copy(
@@ -147,7 +165,19 @@
             )
             swaps[-1].start()
 
-    load_opers.wait()
+    def pump():
+        b = len(swaps) // 2
+        if b < half:
+            for h in range(2):
+                swaps[2 * (b - DEPTH) + h].wait_send()
+            swap(b)
+
+    for b in range(DEPTH):
+        swap(b)
+
+    loads[4].wait()
+    loads[5].wait()
+    loads[6].wait()
     groups = weights.shape[0] // bins_all
     per_group = weights.shape[1] // bins_all
 
@@ -158,6 +188,7 @@
         return carry
 
     lax.fori_loop(0, groups, arrange, 0)
+    pump()
 
     def wait_parm(s):
         pltpu.make_async_copy(parm.at[s], parm.at[s], parm_recv.at[s]).wait()
@@ -189,6 +220,7 @@
                 preferred_element_type=jnp.float32,
             )
         source[b] = total.reshape(planes_src, rows_y, grid_z)
+        pump()
 
     halos = [[None, None] for _ in range(half)]
 
@@ -282,7 +314,7 @@
 
     lax.fori_loop(0, cells // 2, update, 0)
 
-    for copy in parms + swaps:
+    for copy in parms + swaps[2 * (half - DEPTH) :]:
         copy.wait_send()
     for b in range(half):
         for s in range(2):
@@ -302,20 +334,16 @@
         cells = planes * (rows_y // ba_count)
         per_group = 4
         vmem = pl.BlockSpec(memory_space=pltpu.VMEM)
-        anywhere = pl.BlockSpec(memory_space=pl.ANY)
         out = pl.pallas_call(
             functools.partial(kernel, gx_count, ba_count),
             out_shape=jax.ShapeDtypeStruct((bins_all * cells, grid_z), jnp.float32),
-            in_specs=[
-                pl.BlockSpec(memory_space=pltpu.SMEM),
-                anywhere,
-                vmem,
-                vmem,
-                vmem,
-                anywhere,
-            ],
+            in_specs=[pl.BlockSpec(memory_space=pltpu.HBM)] * 6,
             out_specs=vmem,
             scratch_shapes=[
+                pltpu.SMEM((bins_dev,), jnp.float32),
+                pltpu.VMEM((1, remnants), jnp.int32),
+                pltpu.VMEM((bins_dev, remnants), jnp.float32),
+                pltpu.VMEM((cells, grid_z), jnp.int32),
                 pltpu.VMEM(density.shape, jnp.float32),
                 pltpu.VMEM((2, half, planes, rows_y, grid_z), jnp.int16),
                 pltpu.VMEM((2, half, planes, rows_y, grid_z), jnp.int16),
@@ -328,7 +356,7 @@
                 pltpu.VMEM((bins_all * cells, grid_z), jnp.float32),
                 pltpu.VMEM(operators.shape, jnp.bfloat16),
                 pltpu.VMEM((classes // per_group * bins_all, per_group * bins_all), jnp.bfloat16),
-                pltpu.SemaphoreType.DMA((3,)),
+                pltpu.SemaphoreType.DMA((7,)),
                 pltpu.SemaphoreType.DMA((2, half)),
                 pltpu.SemaphoreType.DMA((2, half)),
                 pltpu.SemaphoreType.DMA((2,)),
@@ -338,14 +366,21 @@
                 pltpu.SemaphoreType.DMA,
                 pltpu.SemaphoreType.DMA,
             ],
-            compiler_params=pltpu.CompilerParams(collective_id=0, has_side_effects=True),
+            compiler_params=pltpu.CompilerParams(
+                collective_id=0, has_side_effects=True, vmem_limit_bytes=16 * 2**20
+            ),
         )(
-            diffusivity,
-            density,
-            positions.reshape(1, remnants),
-            spectrum.T,
-            cell_class.reshape(cells, grid_z),
-            operators,
+            *[
+                pltpu.with_memory_space_constraint(operand, pltpu.HBM)
+                for operand in (
+                    diffusivity,
+                    density,
+                    positions.reshape(1, remnants),
+                    spectrum.T,
+                    cell_class.reshape(cells, grid_z),
+                    operators,
+                )
+            ]
         )
         return out.reshape(bins_all, planes, rows_y // ba_count, grid_z)
 

time: 41.8 us -> 39 us (0.933)
  Pallas kernels: 39.7 us -> 38.1 us
  local copies, waits for them, and re-layouts: 1.87 us -> 0.8 us
    pallas_call x1, Pallas kernels: 39.7 us -> 38.1 us  [step(): pl.pallas_call(functools.partial(kernel, gx_count, ba_count), out_shape=j...]
    unnamed x1, local copies, waits for them, and re-layouts: 1.87 us -> 0.8 us
where the time goes in v2:
time: 39 us; the launch traced here: 38.9 us
  Pallas kernels  38.1 us (98%)
  local copies, waits for them, and re-layouts  0.8 us (2%)
    pallas_call x1, Pallas kernels, step(): pl.pallas_call(functools.partial(kernel, gx_count, ba_count), out_shape=j...  38.1 us
    unnamed x1, local copies, waits for them, and re-layouts  0.8 us

profile of v2, /device:TPU:1, one launch (start us, length us, event | category | flops | bytes accessed | tf_op | source)
XLA Modules:
  0.0 38.9 jit_solution(4588381173995373902)
XLA Ops:
  0.0 38.1 %shard_map.64 = f32[1024,128]{1,0:T(8,128)S(1)} custom-call(f32[8]{0:T(128)} %diff_hbm.1, f32[8,2,64,128]{3,2,1,0:T(8,128)} %density_ref.1, s32[1,512]{1,0:T(1,128)} %bitcast.7, f32[8,512]{1,0:T(8,128)} %bitcast.5, s32[16,128]{1,0:T(8,128)} %bitcast.6, bf16[64,64,64]{2,1,0:T(8,128)(2,1)} %oper_ref.1), custom_call_target="tpu_custom_call" | custom-call | tf_op jit(solution)/shard_map/pallas_call | solution.py:337
  38.1 0.8 %copy.8 = f32[64,2,8,128]{3,2,1,0:T(8,128)} copy(f32[64,2,8,128]{3,2,1,0:T(8,128)S(1)} %bitcast.4) | data formatting | bytes 1048576

commit v3 on v2

--- a/solution.py
+++ b/solution.py
@@ -12,8 +12,6 @@
 LOW = 0.1
 STEPS = 32767.0
 BIAS = 32768
-
-DEPTH = 2
 
 
 def encode(rho):
@@ -57,8 +55,10 @@
     rounded,
     gathered,
     wide,
+    sums,
     opers,
     weights,
+    chunk_weights,
     load_sem,
     swap_send,
     swap_recv,
@@ -73,7 +73,7 @@
     half = bins_dev // 2
     ring = 2 * ba_count
     rows_dev = rows_y // ba_count
-    bins_all = gathered.shape[0]
+    bins_all = opers.shape[1]
     remnants = pos_ref.shape[1]
     part = remnants // 2
     gx = lax.axis_index("gx")
@@ -105,17 +105,18 @@
     loads = [
         pltpu.make_async_copy(diff_hbm, diff_ref, load_sem.at[0]),
         pltpu.make_async_copy(spec_hbm, spec_ref, load_sem.at[1]),
+        pltpu.make_async_copy(pos_hbm, pos_ref, load_sem.at[2]),
+        pltpu.make_async_copy(oper_ref, opers, load_sem.at[3]),
+        pltpu.make_async_copy(class_hbm, class_ref, load_sem.at[4]),
+    ]
+    loads += [
         pltpu.make_async_copy(
-            density_ref.at[pl.ds(0, half)], dens.at[pl.ds(0, half)], load_sem.at[2]
-        ),
-        pltpu.make_async_copy(
-            density_ref.at[pl.ds(half, half)], dens.at[pl.ds(half, half)], load_sem.at[3]
-        ),
-        pltpu.make_async_copy(pos_hbm, pos_ref, load_sem.at[4]),
-        pltpu.make_async_copy(oper_ref, opers, load_sem.at[5]),
-        pltpu.make_async_copy(class_hbm, class_ref, load_sem.at[6]),
+            density_ref.at[h * half + b], dens.at[h * half + b], load_sem.at[5 + h * half + b]
+        )
+        for b in range(half)
+        for h in range(2)
     ]
-    for copy in loads:
+    for copy in loads[:2] + loads[5:] + loads[2:5]:
         copy.start()
 
     loads[0].wait()
@@ -129,14 +130,30 @@
         for b in range(half):
             value = jnp.where(bin_row == b, diff_ref[h * half + b], value)
         parm_out[h, :, part:] = value
-    for h in range(2):
-        loads[2 + h].wait()
-        for b in range(half):
+    swaps = []
+
+    def encode_chunk(b):
+        for h in range(2):
+            loads[5 + 2 * b + h].wait()
             stage[h, b] = encode(dens[h * half + b]).astype(jnp.int16)
 
+    def swap(b):
+        for h in range(2):
+            swaps.append(
+                pltpu.make_async_remote_copy(
+                    src_ref=stage.at[h, b],
+                    dst_ref=held.at[side, b],
+                    send_sem=swap_send.at[h, b],
+                    recv_sem=swap_recv.at[side, b],
+                    device_id=(column + h, meet),
+                    device_id_type=MESH,
+                )
+            )
+            swaps[-1].start()
+
+    encode_chunk(0)
     pl.semaphore_wait(barrier, greetings)
 
-    swaps = []
     parms = []
     for h in range(2):
         target = (column + h, meet)
@@ -151,50 +168,26 @@
             )
         )
         parms[h].start()
-    def swap(b):
-        for h in range(2):
-            swaps.append(
-                pltpu.make_async_remote_copy(
-                    src_ref=stage.at[h, b],
-                    dst_ref=held.at[side, b],
-                    send_sem=swap_send.at[h, b],
-                    recv_sem=swap_recv.at[side, b],
-                    device_id=(column + h, meet),
-                    device_id_type=MESH,
-                )
-            )
-            swaps[-1].start()
-
-    def pump():
-        b = len(swaps) // 2
-        if b < half:
-            for h in range(2):
-                swaps[2 * (b - DEPTH) + h].wait_send()
-            swap(b)
-
-    for b in range(DEPTH):
-        swap(b)
-
+    swap(0)
+    for b in range(1, half):
+        encode_chunk(b)
+
+    loads[2].wait()
+    loads[3].wait()
     loads[4].wait()
-    loads[5].wait()
-    loads[6].wait()
-    groups = weights.shape[0] // bins_all
-    per_group = weights.shape[1] // bins_all
+    quad = weights.shape[1] // bins_all
+    quads = weights.shape[0] // bins_all
 
     def arrange(a, carry):
         weights[pl.ds(pl.multiple_of(a * bins_all, bins_all), bins_all), :] = jnp.concatenate(
-            [opers[a * per_group + j] for j in range(per_group)], axis=1
+            [opers[a * quad + j] for j in range(quad)], axis=1
         )
         return carry
 
-    lax.fori_loop(0, groups, arrange, 0)
-    pump()
-
-    def wait_parm(s):
-        pltpu.make_async_copy(parm.at[s], parm.at[s], parm_recv.at[s]).wait()
-
-    wait_parm(0)
-    wait_parm(1)
+    lax.fori_loop(0, quads // 2, arrange, 0)
+    swap(1)
+    lax.fori_loop(quads // 2, quads, arrange, 0)
+
     planes_col = 2 * planes
     planes_src = planes_col + 2
     pos = pos_ref[...]
@@ -205,22 +198,33 @@
     pos_x = lax.rem(pos_x + (width + 1) - column * planes, width)
     pos_row = pos_x * rows_y + pos_y
     is_row = lax.broadcasted_iota(jnp.int32, (planes_src * rows_y, remnants), 0) == pos_row
+    is_row = jnp.where(is_row, 1.0, 0.0).astype(jnp.bfloat16)
     is_z = lax.broadcasted_iota(jnp.int32, (grid_z, remnants), 0) == pos_z
-    is_z = jnp.where(is_z, 1.0, 0.0).astype(jnp.bfloat16)
-    for b in range(half):
-        spec = jnp.concatenate([parm[0, b : b + 1, 0:part], parm[1, b : b + 1, 0:part]], axis=1)
-        high = spec.astype(jnp.bfloat16).astype(jnp.float32)
-        low = spec - high
-        total = jnp.zeros((planes_src * rows_y, grid_z), jnp.float32)
+    swap(2)
+    for s in range(2):
+        pltpu.make_async_copy(parm.at[s], parm.at[s], parm_recv.at[s]).wait()
+    swap(3)
+    spec = jnp.concatenate([parm[0, :, 0:part], parm[1, :, 0:part]], axis=1)
+    high = spec.astype(jnp.bfloat16).astype(jnp.float32)
+    low = spec - high
+
+    def inject(pair):
+        total = jnp.zeros((planes_src * rows_y, 2 * grid_z), jnp.float32)
         for piece in (high, low):
+            placed = [
+                jnp.where(is_z, piece[b : b + 1], 0.0).astype(jnp.bfloat16)
+                for b in (2 * pair, 2 * pair + 1)
+            ]
             total += lax.dot_general(
-                jnp.where(is_row, piece, 0.0).astype(jnp.bfloat16),
-                is_z,
+                is_row,
+                jnp.concatenate(placed, axis=0),
                 (((1,), (1,)), ((), ())),
                 preferred_element_type=jnp.float32,
             )
-        source[b] = total.reshape(planes_src, rows_y, grid_z)
-        pump()
+        for j in range(2):
+            source[2 * pair + j] = total[:, j * grid_z : (j + 1) * grid_z].reshape(
+                planes_src, rows_y, grid_z
+            )
 
     halos = [[None, None] for _ in range(half)]
 
@@ -236,6 +240,35 @@
                 device_id_type=MESH,
             )
             halos[b][s].start()
+
+    low_classes = chunk_weights.shape[2] // ring
+    high_classes = chunk_weights.shape[1] // bins_all
+
+    def regroup():
+        size = weights.shape[1]
+        k = lax.broadcasted_iota(jnp.int32, (size, size), 0)
+        n = lax.broadcasted_iota(jnp.int32, (size, size), 1)
+        wanted = (n // bins_all) + half * lax.rem(n, ring)
+        pick = (k // bins_all == lax.rem(n, bins_all) // ring) & (lax.rem(k, bins_all) == wanted)
+        pick = jnp.where(pick, 1.0, 0.0).astype(jnp.bfloat16)
+        per_high = low_classes // quad
+
+        def one(a, carry):
+            rows = pl.ds(pl.multiple_of(a * per_high * bins_all, bins_all), per_high * bins_all)
+            picked = jnp.dot(weights[rows, :], pick, preferred_element_type=jnp.float32)
+            picked = picked.astype(jnp.bfloat16)
+            place = pl.ds(pl.multiple_of(a * bins_all, bins_all), bins_all)
+            for b in range(half):
+                chunk_weights[b, place, :] = jnp.concatenate(
+                    [
+                        picked[t * bins_all : (t + 1) * bins_all, b * bins_all : (b + 1) * bins_all]
+                        for t in range(per_high)
+                    ],
+                    axis=1,
+                )
+            return carry
+
+        lax.fori_loop(0, high_classes, one, 0)
 
     def diffuse(b):
         for s in range(2):
@@ -266,55 +299,74 @@
     group = 2 * meet + side
 
     def spread(b):
-        slot = gathered.at[group * half + b]
+        slot = gathered.at[b, group]
         for offset in list(range(ring // 2, ring)) + list(range(1, ring // 2)):
             peer = lax.rem(me + offset, ring)
             pltpu.make_async_remote_copy(
                 src_ref=rounded.at[b, peer],
                 dst_ref=slot,
                 send_sem=spread_send,
-                recv_sem=spread_recv,
+                recv_sem=spread_recv.at[b],
                 device_id=(column + peer // ba_count, lax.rem(peer, ba_count)),
                 device_id_type=MESH,
             ).start()
-        pltpu.make_async_copy(rounded.at[b, me], slot, spread_recv).start()
+        pltpu.make_async_copy(rounded.at[b, me], slot, spread_recv.at[b]).start()
 
     forward(0)
-    for b in range(half):
-        if b + 1 < half:
-            forward(b + 1)
+    inject(0)
+    forward(1)
+    inject(1)
+    forward(2)
+    regroup()
+    diffuse(0)
+    spread(0)
+    forward(3)
+    for b in range(1, half):
         diffuse(b)
         spread(b)
 
-    pltpu.make_async_copy(gathered, gathered, spread_recv).wait()
-
-    wide[...] = gathered[...].astype(jnp.float32).reshape(wide.shape)
     cells = planes * rows_dev
 
-    def update(step, carry):
-        first_row = 2 * step
-        values = jnp.concatenate(
-            [wide[pl.ds(first_row + j, bins_all, stride=cells), :] for j in range(2)], axis=1
-        )
-        classes = jnp.concatenate([class_ref[pl.ds(first_row + j, 1), :] for j in range(2)], axis=1)
-        within = lax.rem(classes, per_group)
-        outer = classes // per_group
-        stacked = jnp.concatenate(
-            [jnp.where(within == j, values, 0.0) for j in range(per_group)], axis=0
-        ).astype(jnp.bfloat16)
-        products = jnp.dot(weights[...], stacked, preferred_element_type=jnp.float32)
-        result = products[0:bins_all]
-        for a in range(1, groups):
-            result = jnp.where(outer == a, products[a * bins_all : (a + 1) * bins_all], result)
-        for j in range(2):
-            out_ref[pl.ds(first_row + j, bins_all, stride=cells), :] = result[
-                :, j * grid_z : (j + 1) * grid_z
-            ]
-        return carry
-
-    lax.fori_loop(0, cells // 2, update, 0)
-
-    for copy in parms + swaps[2 * (half - DEPTH) :]:
+    def update(b):
+        pltpu.make_async_copy(gathered.at[b], gathered.at[b], spread_recv.at[b]).wait()
+        wide[...] = gathered[b].astype(jnp.float32).reshape(wide.shape)
+
+        def pair(step, carry):
+            first_row = 2 * step
+            values = jnp.concatenate(
+                [wide[pl.ds(first_row + j, ring, stride=cells), :] for j in range(2)], axis=1
+            )
+            classes = jnp.concatenate(
+                [class_ref[pl.ds(first_row + j, 1), :] for j in range(2)], axis=1
+            )
+            low_class = lax.rem(classes, low_classes)
+            high_class = classes // low_classes
+            stacked = jnp.concatenate(
+                [jnp.where(low_class == j, values, 0.0) for j in range(low_classes)], axis=0
+            ).astype(jnp.bfloat16)
+            products = jnp.dot(chunk_weights[b], stacked, preferred_element_type=jnp.float32)
+            result = products[0:bins_all]
+            for a in range(1, high_classes):
+                result = jnp.where(
+                    high_class == a, products[a * bins_all : (a + 1) * bins_all], result
+                )
+            if b > 0:
+                result += sums[step]
+            if b < half - 1:
+                sums[step] = result
+            else:
+                for j in range(2):
+                    out_ref[pl.ds(first_row + j, bins_all, stride=cells), :] = result[
+                        :, j * grid_z : (j + 1) * grid_z
+                    ]
+            return carry
+
+        lax.fori_loop(0, cells // 2, pair, 0, unroll=8)
+
+    for b in range(half):
+        update(b)
+
+    for copy in parms + swaps:
         copy.wait_send()
     for b in range(half):
         for s in range(2):
@@ -332,7 +384,7 @@
         remnants = positions.shape[0]
         half = bins_dev // 2
         cells = planes * (rows_y // ba_count)
-        per_group = 4
+        quad, low_classes = 4, 16
         vmem = pl.BlockSpec(memory_space=pltpu.VMEM)
         out = pl.pallas_call(
             functools.partial(kernel, gx_count, ba_count),
@@ -352,11 +404,13 @@
                 pltpu.VMEM((2, half, remnants // 2 + grid_z), jnp.float32),
                 pltpu.VMEM((half, 2 * planes + 2, rows_y, grid_z), jnp.float32),
                 pltpu.VMEM((half, 2 * ba_count, cells, grid_z), jnp.bfloat16),
-                pltpu.VMEM((bins_all, cells, grid_z), jnp.bfloat16),
-                pltpu.VMEM((bins_all * cells, grid_z), jnp.float32),
+                pltpu.VMEM((half, 2 * ba_count, cells, grid_z), jnp.bfloat16),
+                pltpu.VMEM((2 * ba_count * cells, grid_z), jnp.float32),
+                pltpu.VMEM((cells // 2, bins_all, 2 * grid_z), jnp.float32),
                 pltpu.VMEM(operators.shape, jnp.bfloat16),
-                pltpu.VMEM((classes // per_group * bins_all, per_group * bins_all), jnp.bfloat16),
-                pltpu.SemaphoreType.DMA((7,)),
+                pltpu.VMEM((classes // quad * bins_all, quad * bins_all), jnp.bfloat16),
+                pltpu.VMEM((half, classes // low_classes * bins_all, low_classes * 2 * ba_count), jnp.bfloat16),
+                pltpu.SemaphoreType.DMA((5 + bins_dev,)),
                 pltpu.SemaphoreType.DMA((2, half)),
                 pltpu.SemaphoreType.DMA((2, half)),
                 pltpu.SemaphoreType.DMA((2,)),
@@ -364,7 +418,7 @@
                 pltpu.SemaphoreType.DMA((2, half)),
                 pltpu.SemaphoreType.DMA((2, half)),
                 pltpu.SemaphoreType.DMA,
-                pltpu.SemaphoreType.DMA,
+                pltpu.SemaphoreType.DMA((half,)),
             ],
             compiler_params=pltpu.CompilerParams(
                 collective_id=0, has_side_effects=True, vmem_limit_bytes=16 * 2**20

time: 39 us -> 35 us (0.90)
  Pallas kernels: 38.1 us -> 34.1 us
    pallas_call x1, Pallas kernels: 38.1 us -> 34.1 us  [step(): pl.pallas_call(functools.partial(kernel, gx_count, ba_count), out_shape=j...]
where the time goes in v3:
time: 35 us; the launch traced here: 34.9 us
  Pallas kernels  34.1 us (97%)
  local copies, waits for them, and re-layouts  0.8 us (2%)
    pallas_call x1, Pallas kernels, step(): pl.pallas_call(functools.partial(kernel, gx_count, ba_count), out_shape=j...  34.1 us
    unnamed x1, local copies, waits for them, and re-layouts  0.8 us

profile of v3, /device:TPU:1, one launch (start us, length us, event | category | flops | bytes accessed | tf_op | source)
XLA Modules:
  0.0 34.9 jit_solution(14567413548631123341)
XLA Ops:
  0.0 34.1 %shard_map.64 = f32[1024,128]{1,0:T(8,128)S(1)} custom-call(f32[8]{0:T(128)} %diff_hbm.1, f32[8,2,64,128]{3,2,1,0:T(8,128)} %density_ref.1, s32[1,512]{1,0:T(1,128)} %bitcast.7, f32[8,512]{1,0:T(8,128)} %bitcast.5, s32[16,128]{1,0:T(8,128)} %bitcast.6, bf16[64,64,64]{2,1,0:T(8,128)(2,1)} %oper_ref.1), custom_call_target="tpu_custom_call" | custom-call | tf_op jit(solution)/shard_map/pallas_call | solution.py:389
  34.1 0.8 %copy.8 = f32[64,2,8,128]{3,2,1,0:T(8,128)} copy(f32[64,2,8,128]{3,2,1,0:T(8,128)S(1)} %bitcast.4) | data formatting | bytes 1048576

commit v4 on v3

--- a/solution.py
+++ b/solution.py
@@ -297,17 +297,20 @@
             rounded[b, pl.ds(s * ba_count, ba_count)] = block.astype(jnp.bfloat16)
 
     group = 2 * meet + side
+    peers = []
+    for offset in sorted(range(1, ring), key=lambda o: -min(o, ring - o)):
+        peer = lax.rem(me + offset, ring)
+        peers.append((peer, (column + peer // ba_count, lax.rem(peer, ba_count))))
 
     def spread(b):
         slot = gathered.at[b, group]
-        for offset in list(range(ring // 2, ring)) + list(range(1, ring // 2)):
-            peer = lax.rem(me + offset, ring)
+        for peer, place in peers:
             pltpu.make_async_remote_copy(
                 src_ref=rounded.at[b, peer],
                 dst_ref=slot,
                 send_sem=spread_send,
                 recv_sem=spread_recv.at[b],
-                device_id=(column + peer // ba_count, lax.rem(peer, ba_count)),
+                device_id=place,
                 device_id_type=MESH,
             ).start()
         pltpu.make_async_copy(rounded.at[b, me], slot, spread_recv.at[b]).start()
@@ -317,13 +320,16 @@
     forward(1)
     inject(1)
     forward(2)
-    regroup()
+    forward(3)
     diffuse(0)
     spread(0)
-    forward(3)
-    for b in range(1, half):
-        diffuse(b)
-        spread(b)
+    diffuse(1)
+    spread(1)
+    diffuse(2)
+    spread(2)
+    diffuse(3)
+    spread(3)
+    regroup()
 
     cells = planes * rows_dev
 

time: 35 us -> 34.6 us (0.989)
  Pallas kernels: 34.1 us -> 33.6 us
    pallas_call x1, Pallas kernels: 34.1 us -> 33.6 us  [step(): pl.pallas_call(functools.partial(kernel, gx_count, ba_count), out_shape=j...]
where the time goes in v4:
time: 34.6 us; the launch traced here: 34.4 us
  Pallas kernels  33.6 us (97%)
  local copies, waits for them, and re-layouts  0.8 us (2%)
    pallas_call x1, Pallas kernels, step(): pl.pallas_call(functools.partial(kernel, gx_count, ba_count), out_shape=j...  33.6 us
    unnamed x1, local copies, waits for them, and re-layouts  0.8 us

profile of v4, /device:TPU:1, one launch (start us, length us, event | category | flops | bytes accessed | tf_op | source)
XLA Modules:
  0.0 34.4 jit_solution(15258339423248482893)
XLA Ops:
  0.0 33.6 %shard_map.64 = f32[1024,128]{1,0:T(8,128)S(1)} custom-call(f32[8]{0:T(128)} %diff_hbm.1, f32[8,2,64,128]{3,2,1,0:T(8,128)} %density_ref.1, s32[1,512]{1,0:T(1,128)} %bitcast.7, f32[8,512]{1,0:T(8,128)} %bitcast.5, s32[16,128]{1,0:T(8,128)} %bitcast.6, bf16[64,64,64]{2,1,0:T(8,128)(2,1)} %oper_ref.1), custom_call_target="tpu_custom_call" | custom-call | tf_op jit(solution)/shard_map/pallas_call | solution.py:395
  33.6 0.8 %copy.8 = f32[64,2,8,128]{3,2,1,0:T(8,128)} copy(f32[64,2,8,128]{3,2,1,0:T(8,128)S(1)} %bitcast.4) | data formatting | bytes 1048576

commit v5 on v4

--- a/solution.py
+++ b/solution.py
@@ -177,16 +177,7 @@
     loads[4].wait()
     quad = weights.shape[1] // bins_all
     quads = weights.shape[0] // bins_all
-
-    def arrange(a, carry):
-        weights[pl.ds(pl.multiple_of(a * bins_all, bins_all), bins_all), :] = jnp.concatenate(
-            [opers[a * quad + j] for j in range(quad)], axis=1
-        )
-        return carry
-
-    lax.fori_loop(0, quads // 2, arrange, 0)
     swap(1)
-    lax.fori_loop(quads // 2, quads, arrange, 0)
 
     planes_col = 2 * planes
     planes_src = planes_col + 2
@@ -315,10 +306,10 @@
             ).start()
         pltpu.make_async_copy(rounded.at[b, me], slot, spread_recv.at[b]).start()
 
+    inject(0)
     forward(0)
-    inject(0)
+    inject(1)
     forward(1)
-    inject(1)
     forward(2)
     forward(3)
     diffuse(0)
@@ -329,6 +320,14 @@
     spread(2)
     diffuse(3)
     spread(3)
+
+    def arrange(a, carry):
+        weights[pl.ds(pl.multiple_of(a * bins_all, bins_all), bins_all), :] = jnp.concatenate(
+            [opers[a * quad + j] for j in range(quad)], axis=1
+        )
+        return carry
+
+    lax.fori_loop(0, quads, arrange, 0, unroll=4)
     regroup()
 
     cells = planes * rows_dev

time: 34.6 us -> 34.2 us (0.988)
  no operation moved by 1% of the time
where the time goes in v5:
time: 34.2 us; the launch traced here: 34.1 us
  Pallas kernels  33.3 us (97%)
  local copies, waits for them, and re-layouts  0.8 us (2%)
    pallas_call x1, Pallas kernels, step(): pl.pallas_call(functools.partial(kernel, gx_count, ba_count), out_shape=j...  33.3 us
    unnamed x1, local copies, waits for them, and re-layouts  0.8 us

profile of v5, /device:TPU:1, one launch (start us, length us, event | category | flops | bytes accessed | tf_op | source)
XLA Modules:
  0.0 34.1 jit_solution(10698819665465321286)
XLA Ops:
  0.0 33.3 %shard_map.64 = f32[1024,128]{1,0:T(8,128)S(1)} custom-call(f32[8]{0:T(128)} %diff_hbm.1, f32[8,2,64,128]{3,2,1,0:T(8,128)} %density_ref.1, s32[1,512]{1,0:T(1,128)} %bitcast.7, f32[8,512]{1,0:T(8,128)} %bitcast.5, s32[16,128]{1,0:T(8,128)} %bitcast.6, bf16[64,64,64]{2,1,0:T(8,128)(2,1)} %oper_ref.1), custom_call_target="tpu_custom_call" | custom-call | tf_op jit(solution)/shard_map/pallas_call | solution.py:394
  33.3 0.8 %copy.8 = f32[64,2,8,128]{3,2,1,0:T(8,128)} copy(f32[64,2,8,128]{3,2,1,0:T(8,128)S(1)} %bitcast.4) | data formatting | bytes 1048576

commit v6 on v5

--- a/solution.py
+++ b/solution.py
@@ -52,6 +52,7 @@
     parm_out,
     parm,
     source,
+    inner,
     rounded,
     gathered,
     wide,
@@ -261,19 +262,39 @@
 
         lax.fori_loop(0, high_classes, one, 0)
 
+    def prepare(b):
+        rate = parm[0, b : b + 1, part:]
+        centre = 1.0 - 6.0 * rate
+        fields = [decode(held[s, b, p]) for s in range(2) for p in range(planes)]
+        for p in range(planes_col):
+            around = yz_sum(fields[p])
+            if p > 0:
+                around += fields[p - 1]
+            if p + 1 < planes_col:
+                around += fields[p + 1]
+            inner[b, p] = centre * fields[p] + rate * around + source[b, p + 1]
+
     def diffuse(b):
         for s in range(2):
             halos[b][s].wait_recv()
         rate = parm[0, b : b + 1, part:]
         centre = 1.0 - 6.0 * rate
-        fields = [decode(halo[1, b, p]) for p in range(planes)]
-        fields += [decode(held[s, b, p]) for s in range(2) for p in range(planes)]
-        fields += [decode(halo[0, b, p]) for p in range(planes)]
+        before = [decode(halo[1, b, p]) for p in range(planes)]
+        after = [decode(halo[0, b, p]) for p in range(planes)]
         sources = [source[b, p] for p in range(planes_src)]
         first = [
-            centre * fields[p + 1] + rate * (fields[p] + fields[p + 2] + yz_sum(fields[p + 1])) + sources[p]
-            for p in range(planes_src)
+            centre * before[-1]
+            + rate * (before[-2] + decode(held[0, b, 0]) + yz_sum(before[-1]))
+            + sources[0]
         ]
+        first += [inner[b, p] for p in range(planes_col)]
+        first[1] += rate * before[-1]
+        first[planes_col] += rate * after[0]
+        first.append(
+            centre * after[0]
+            + rate * (decode(held[1, b, planes - 1]) + after[1] + yz_sum(after[0]))
+            + sources[planes_src - 1]
+        )
         second = [
             centre * first[p + 1]
             + rate * (first[p] + first[p + 2] + yz_sum(first[p + 1]))
@@ -308,10 +329,14 @@
 
     inject(0)
     forward(0)
+    prepare(0)
     inject(1)
     forward(1)
+    prepare(1)
     forward(2)
+    prepare(2)
     forward(3)
+    prepare(3)
     diffuse(0)
     spread(0)
     diffuse(1)
@@ -408,6 +433,7 @@
                 pltpu.VMEM((2, half, remnants // 2 + grid_z), jnp.float32),
                 pltpu.VMEM((2, half, remnants // 2 + grid_z), jnp.float32),
                 pltpu.VMEM((half, 2 * planes + 2, rows_y, grid_z), jnp.float32),
+                pltpu.VMEM((half, 2 * planes, rows_y, grid_z), jnp.float32),
                 pltpu.VMEM((half, 2 * ba_count, cells, grid_z), jnp.bfloat16),
                 pltpu.VMEM((half, 2 * ba_count, cells, grid_z), jnp.bfloat16),
                 pltpu.VMEM((2 * ba_count * cells, grid_z), jnp.float32),

time: 34.2 us -> 34.2 us (level)
  no operation moved by 1% of the time
where the time goes in v6:
time: 34.2 us; the launch traced here: 34 us
  Pallas kernels  33.2 us (97%)
  local copies, waits for them, and re-layouts  0.8 us (2%)
    pallas_call x1, Pallas kernels, step(): pl.pallas_call(functools.partial(kernel, gx_count, ba_count), out_shape=j...  33.2 us
    unnamed x1, local copies, waits for them, and re-layouts  0.8 us

profile of v6, /device:TPU:1, one launch (start us, length us, event | category | flops | bytes accessed | tf_op | source)
XLA Modules:
  0.0 34.0 jit_solution(13404908320791200306)
XLA Ops:
  0.0 33.2 %shard_map.64 = f32[1024,128]{1,0:T(8,128)S(1)} custom-call(f32[8]{0:T(128)} %diff_hbm.1, f32[8,2,64,128]{3,2,1,0:T(8,128)} %density_ref.1, s32[1,512]{1,0:T(1,128)} %bitcast.7, f32[8,512]{1,0:T(8,128)} %bitcast.5, s32[16,128]{1,0:T(8,128)} %bitcast.6, bf16[64,64,64]{2,1,0:T(8,128)(2,1)} %oper_ref.1), custom_call_target="tpu_custom_call" | custom-call | tf_op jit(solution)/shard_map/pallas_call | solution.py:419
  33.2 0.8 %copy.8 = f32[64,2,8,128]{3,2,1,0:T(8,128)} copy(f32[64,2,8,128]{3,2,1,0:T(8,128)S(1)} %bitcast.4) | data formatting | bytes 1048576

commit v7 on v6

--- a/solution.py
+++ b/solution.py
@@ -393,14 +393,14 @@
 
         lax.fori_loop(0, cells // 2, pair, 0, unroll=8)
 
-    for b in range(half):
-        update(b)
-
     for copy in parms + swaps:
         copy.wait_send()
     for b in range(half):
         for s in range(2):
             halos[b][s].wait_send()
+    for b in range(half):
+        update(b)
+
     sent = rounded.at[:, pl.ds(0, ring - 1)]
     pltpu.make_async_copy(sent, sent, spread_send).wait()
 

time: 34.2 us -> 34.1 us (level)
  no operation moved by 1% of the time
where the time goes in v7:
time: 34.1 us; the launch traced here: 34 us
  Pallas kernels  33.2 us (97%)
  local copies, waits for them, and re-layouts  0.8 us (2%)
    pallas_call x1, Pallas kernels, step(): pl.pallas_call(functools.partial(kernel, gx_count, ba_count), out_shape=j...  33.2 us
    unnamed x1, local copies, waits for them, and re-layouts  0.8 us

profile of v7, /device:TPU:1, one launch (start us, length us, event | category | flops | bytes accessed | tf_op | source)
XLA Modules:
  0.0 34.0 jit_solution(15623645601602891009)
XLA Ops:
  0.0 33.2 %shard_map.64 = f32[1024,128]{1,0:T(8,128)S(1)} custom-call(f32[8]{0:T(128)} %diff_hbm.1, f32[8,2,64,128]{3,2,1,0:T(8,128)} %density_ref.1, s32[1,512]{1,0:T(1,128)} %bitcast.7, f32[8,512]{1,0:T(8,128)} %bitcast.5, s32[16,128]{1,0:T(8,128)} %bitcast.6, bf16[64,64,64]{2,1,0:T(8,128)(2,1)} %oper_ref.1), custom_call_target="tpu_custom_call" | custom-call | tf_op jit(solution)/shard_map/pallas_call | solution.py:419
  33.2 0.8 %copy.8 = f32[64,2,8,128]{3,2,1,0:T(8,128)} copy(f32[64,2,8,128]{3,2,1,0:T(8,128)S(1)} %bitcast.4) | data formatting | bytes 1048576

commit v8 on v6

--- a/solution.py
+++ b/solution.py
@@ -192,10 +192,9 @@
     is_row = lax.broadcasted_iota(jnp.int32, (planes_src * rows_y, remnants), 0) == pos_row
     is_row = jnp.where(is_row, 1.0, 0.0).astype(jnp.bfloat16)
     is_z = lax.broadcasted_iota(jnp.int32, (grid_z, remnants), 0) == pos_z
-    swap(2)
     for s in range(2):
         pltpu.make_async_copy(parm.at[s], parm.at[s], parm_recv.at[s]).wait()
-    swap(3)
+    swap(2)
     spec = jnp.concatenate([parm[0, :, 0:part], parm[1, :, 0:part]], axis=1)
     high = spec.astype(jnp.bfloat16).astype(jnp.float32)
     low = spec - high
@@ -328,6 +327,7 @@
         pltpu.make_async_copy(rounded.at[b, me], slot, spread_recv.at[b]).start()
 
     inject(0)
+    swap(3)
     forward(0)
     prepare(0)
     inject(1)

time: 34.2 us -> 34.1 us (level)
  no operation moved by 1% of the time
where the time goes in v8:
time: 34.1 us; the launch traced here: 34 us
  Pallas kernels  33.2 us (97%)
  local copies, waits for them, and re-layouts  0.8 us (2%)
    pallas_call x1, Pallas kernels, step(): pl.pallas_call(functools.partial(kernel, gx_count, ba_count), out_shape=j...  33.2 us
    unnamed x1, local copies, waits for them, and re-layouts  0.8 us

profile of v8, /device:TPU:1, one launch (start us, length us, event | category | flops | bytes accessed | tf_op | source)
XLA Modules:
  0.0 34.0 jit_solution(13044041553511373076)
XLA Ops:
  0.0 33.2 %shard_map.64 = f32[1024,128]{1,0:T(8,128)S(1)} custom-call(f32[8]{0:T(128)} %diff_hbm.1, f32[8,2,64,128]{3,2,1,0:T(8,128)} %density_ref.1, s32[1,512]{1,0:T(1,128)} %bitcast.7, f32[8,512]{1,0:T(8,128)} %bitcast.5, s32[16,128]{1,0:T(8,128)} %bitcast.6, bf16[64,64,64]{2,1,0:T(8,128)(2,1)} %oper_ref.1), custom_call_target="tpu_custom_call" | custom-call | tf_op jit(solution)/shard_map/pallas_call | solution.py:419
  33.2 0.8 %copy.8 = f32[64,2,8,128]{3,2,1,0:T(8,128)} copy(f32[64,2,8,128]{3,2,1,0:T(8,128)S(1)} %bitcast.4) | data formatting | bytes 1048576
